TPU v7x, 256 devices: a whole 4x4x8 slice. The times are simulated.
256 devices in a mesh: sta: 64 (over x_lo, z, y), tpl: 4 (over x_hi, core).
Axes of the slice: x: 4 (x_hi: 2, x_lo: 2; x = x_hi * 2 + x_lo), y: 4, z: 8, core: 2. Of those that a mesh axis runs over, the one named last changes fastest.
Arguments:
- waveform: float32 [128, 1536], P('sta', 'tpl'), may hold values from -6 to 6
- fir_taps: float32 [64], replicated, may hold values from -0.75 to 0.75
- templates: bfloat16 [512, 128, 1024], P('tpl', 'sta'), may hold values from -6 to 6
- presence: int32 [512, 128], P('tpl', 'sta'), may hold values from 0 to 1
- moveout: int32 [512, 128], P('tpl', 'sta'), may hold values from 0 to 128
Outputs:
- network_stack: float32 [4, 128, 384], P('tpl', 'sta')
All inputs are finite; a program needn't handle non-finite values.
Results may differ from a plain program's by a relative error of at most 0.0029.
Values may be sent and summed in bfloat16 or wider, within the bound.
A program may use at most 64 MiB of HBM per device.

v0:
```python
import jax
import jax.numpy as jnp
from jax import lax
from jax.sharding import PartitionSpec as P

BLK = 128
SHIFT_MOST = 128


epsilon = 1e-06


def fir_apply(extended, coeffs):
    result = lax.conv_general_dilated(
        extended[:, None, :],
        coeffs[::-1][None, None, :],
        (1,),
        "VALID",
        precision=lax.Precision.HIGHEST,
    )
    return result[:, 0, :]


def hankel(samples):
    leading = samples.shape[:-1]
    row_total = samples.shape[-1] // BLK
    row_blocks = samples.reshape(leading + (row_total, BLK))
    windows = jnp.concatenate([row_blocks[..., :-1, :], row_blocks[..., 1:, :]], axis=-1)
    tiled_win = jnp.tile(windows, (1,) * (windows.ndim - 1) + (BLK + 1,))
    flat_win = tiled_win[..., : BLK * (2 * BLK + 1)]
    return flat_win.reshape(windows.shape[:-1] + (BLK, 2 * BLK + 1))[..., :BLK]


def shards(waveform, fir_taps, templates, presence, moveout):
    tap_count = fir_taps.shape[0]
    gathered = lax.all_gather(waveform, "tpl", axis=1, tiled=True)
    extended = jnp.pad(gathered, ((0, 0), (tap_count - 1, 0)))
    filtered = fir_apply(extended, fir_taps).astype(jnp.bfloat16)
    station_count = filtered.shape[0]
    templ_len = templates.shape[2]
    block_rows = templates.shape[0]
    corr_len = filtered.shape[1] - templ_len
    out_len = corr_len - SHIFT_MOST
    time_blocks = corr_len // BLK
    lag_blocks = templ_len // BLK
    values = filtered.astype(jnp.float32)
    prefix = jnp.concatenate(
        [jnp.zeros((station_count, 1), jnp.float32), jnp.cumsum(values * values, axis=1)], axis=1
    )
    energy = prefix[:, templ_len : templ_len + corr_len] - prefix[:, :corr_len]
    root_energy = jnp.sqrt(energy)
    hankel_rows = hankel(filtered)
    templ_norm = jnp.sqrt(jnp.sum(jnp.square(templates.astype(jnp.float32)), axis=-1) + epsilon)
    lag_index = jnp.arange(out_len, dtype=jnp.int32)
    own_rows = block_rows // lax.axis_size("sta")
    templ_split = templates.reshape(block_rows, station_count, lag_blocks, BLK)
    products = jnp.zeros((station_count, block_rows, time_blocks, BLK), jnp.float32)
    for offset in range(lag_blocks):
        products = products + jnp.einsum(
            "ksb,scbd->skcd",
            templ_split[:, :, offset, :],
            hankel_rows[:, offset : offset + time_blocks],
            preferred_element_type=jnp.float32,
        )
    products = products.reshape(station_count, block_rows, corr_len)
    correlation = products / (templ_norm.T[:, :, None] * root_energy[:, None, :])
    shifts = moveout.T
    weights = presence.T.astype(jnp.float32)
    positions = shifts[:, :, None] + lag_index[None, None, :]
    aligned = jnp.take_along_axis(correlation, positions, axis=2)
    summed = lax.psum(jnp.sum(weights[:, :, None] * aligned, axis=0), "sta")
    dev_index = lax.axis_index("sta")
    stacked = lax.dynamic_slice_in_dim(summed, dev_index * own_rows, own_rows, 0)
    return stacked[None]


def solution(mesh):
    placed = (P("sta", "tpl"), P(), P("tpl", "sta", None), P("tpl", "sta"), P("tpl", "sta"))
    return jax.shard_map(
        shards, mesh=mesh, in_specs=placed, out_specs=P("tpl", "sta", None), check_vma=False
    )
```

profile of v0, /device:TPU:6, one launch (start us, length us, event | category | flops | bytes accessed | tf_op | source)
XLA Modules:
  0.0 1396.6 jit_solution(3931908676046544148)
XLA Ops:
  6.5 0.0 all-reduce.4.cloned.1.call-start
  6.5 6.8 all_gather.3
  13.3 0.1 pad_bitcast_fusion
  13.4 0.1 reshape.59
  13.5 0.1 fusion.15
  13.6 0.1 copy.74
  13.7 0.8 rev.3
  14.5 0.1 copy.75
  14.6 0.0 copy-start.7
  14.6 0.0 copy-start
  14.6 15.2 %fusion.20 = bf16[16,200,1]{0,2,1:T(2,128)(2,1)S(1)} fusion(f32[1,16,263]{1,0,2:T(1,128)S(1)} %copy.74, f32[1,1,64]{1,0,2:T(1,128)S(1)} %copy.75), kind=kOutput, calls=%fused_computation.54 | convolution fusion | flops 2457600 | bytes 23488 | tf_op jit(solution)/shard_map/conv_general_dilated | solution.py:14
  29.9 0.1 copy.76
  29.9 0.0 copy-done.7
  30.0 0.1 reshape.63
  30.1 0.0 copy-done
  30.1 0.7 copy.79
  30.9 1.2 multiply_reduce_fusion
  32.1 0.1 tile.4
  32.2 2.2 tile.10
  34.5 2.1 slice.110
  36.6 6.0 reshape.53
  42.6 0.0 copy-start.6
  42.6 1.4 fusion.18
  44.0 0.0 copy-start.5
  44.0 0.0 copy-start.4
  44.0 0.6 reduce-window.6
  44.6 0.2 slice_reduce_fusion
  44.7 0.2 reduce-window.9
  44.9 0.1 add_bitcast_fusion
  45.0 0.1 fusion.17
  45.1 0.9 sqrt_bitcast_fusion
  46.0 0.1 copy.95
  46.0 0.0 copy-done.6
  46.0 0.2 fusion.2
  46.3 0.0 copy-start.3
  46.3 0.3 fusion.13
  46.6 0.0 copy-start.2
  46.6 0.0 copy-done.5
  46.6 0.3 convolution_add_fusion.6
  46.9 0.0 copy-start.1
  46.9 0.0 copy-done.4
  46.9 0.3 convolution_add_fusion.5
  47.2 0.0 copy-done.3
  47.2 0.3 convolution_add_fusion.4
  47.5 0.1 copy-done.2
  47.6 0.3 convolution_add_fusion.3
  47.8 0.0 copy-done.1
  47.9 0.3 convolution_add_fusion.2
  48.2 0.3 convolution_add_fusion.1
  48.5 0.3 convolution_add_fusion
  48.7 0.2 bitcast_divide_fusion
  49.0 0.0 copy-start.8
  49.0 787.1 %gather_fusion = f32[98304]{0:T(1024)S(1)} fusion(f32[2,128,512]{1,2,0:T(8,128)S(1)} %bitcast_divide_fusion, s32[98304]{0:T(1024)S(1)} %reshape.72), kind=kCustom, calls=%fused_computation | custom fusion | bytes 1966080 | tf_op jit(solution)/shard_map/jit(take_along_axis)/gather | solution.py:70
  836.1 0.1 reshape.75
  836.2 0.0 copy-done.8
  836.2 0.9 multiply_reduce_fusion.1
  837.1 0.0 all-reduce.4.cloned.1.call-update
  837.1 551.3 %all-reduce.4.cloned.1.call-done = f32[128,384]{1,0:T(8,128)} async-done(((f32[128,384]{1,0:T(8,128)}), f32[128,384]{1,0:T(8,128)}) %all-reduce.4.cloned.1.call-update) | async-done | bytes 196624 | tf_op jit(solution)/shard_map/psum | solution.py:71
  1388.4 1.3 dynamic-slice_bitcast_fusion
  (12 shorter events, 0.1 us)
Async XLA Ops:
  6.5 1381.9 %all-reduce.4.cloned.1.call-start = ((), (), s32[]{:S(2)}) async-start(), calls=%async_computation | async-start | bytes 393216 | tf_op jit(solution)/shard_map/psum | solution.py:71
  14.6 15.3 %copy-start.7 = (pred[16,200,1]{1,0,2:T(8,128)(4,1)S(1)}, pred[16,200,1]{1,0,2:T(8,128)(4,1)}, u32[]{:S(2)}) copy-start(pred[16,200,1]{1,0,2:T(8,128)(4,1)} %constant.49) | copy-start | bytes 9604
  14.6 15.5 %copy-start = (bf16[128,2,1024]{2,1,0:T(2,128)(2,1)S(1)}, bf16[128,2,1024]{2,1,0:T(2,128)(2,1)}, u32[]{:S(2)}) copy-start(bf16[128,2,1024]{2,1,0:T(2,128)(2,1)} %param.7) | copy-start | bytes 1572868
  42.6 3.4 copy-start.6
  44.0 2.6 copy-start.5
  44.0 2.9 copy-start.4
  46.3 1.0 copy-start.3
  46.6 1.0 copy-start.2
  46.9 1.0 copy-start.1
  49.0 787.2 %copy-start.8 = (s32[128,2]{0,1:T(2,128)S(1)}, s32[128,2]{0,1:T(2,128)}, u32[]{:S(2)}) copy-start(s32[128,2]{0,1:T(2,128)} %param.8) | copy-start | bytes 3076
Sparse Core Ops, SparseCore 0:
  837.3 551.1 all-reduce.3
where the time goes:
time: 1400 us
  local copies, waits for them, and re-layouts  803 us (57%)
  waiting for transfers between devices  551 us (39%)
  matrix products  17.5 us (1%)
    gather x3, local copies, waits for them, and re-layouts, shards(): aligned = jnp.take_along_axis(correlation, positions, axis=2)  787 us
    psum x1, waiting for transfers between devices, shards(): summed = lax.psum(jnp.sum(weights[:, :, None] * aligned, axis=0), 'sta')  551 us
  transfers between devices with their start and end apart: 1, of which 1 were waited for; matrix products, arithmetic and copies ran while one was open for 0% of the time, Pallas kernels for 0%

commit v1 on v0

v1 whole, which is shorter than its diff:
```python
import functools

import jax
import jax.numpy as jnp
from jax import lax
from jax.experimental import pallas as pl
from jax.experimental.pallas import tpu as pltpu
from jax.sharding import PartitionSpec as P

BLK = 128
SHIFT_MOST = 128
EPSILON = 1e-06
MESH = pl.DeviceIdType.MESH


def lane_gather(values, index):
    return jnp.take_along_axis(values, index, axis=1, mode="promise_in_bounds")


def sta_offsets(n_sta):
    dims = (2, 8, 4) if n_sta == 64 else (1, n_sta, 1)
    steps = [
        (dx, dz, dy) for dx in range(dims[0]) for dz in range(dims[1]) for dy in range(dims[2])
    ][1:]

    def hops(step):
        return sum(min(d, n - d) for d, n in zip(step, dims))

    return dims, sorted(steps, key=lambda step: -hops(step))


def peer(me, step, dims):
    x, rest = me // (dims[1] * dims[2]), me % (dims[1] * dims[2])
    z, y = rest // dims[2], rest % dims[2]
    x = (x + step[0]) % dims[0]
    z = (z + step[1]) % dims[1]
    y = (y + step[2]) % dims[2]
    return (x * dims[1] + z) * dims[2] + y


def kernel(
    n_sta,
    n_tpl,
    wave_ref,
    fir_ref,
    tpl_ref,
    pres_ref,
    mov_ref,
    out_ref,
    wave_buf,
    tpl_raw,
    rows32,
    tpl_split,
    send_buf,
    recv_buf,
    local_sem,
    wave_send,
    wave_recv,
    stack_send,
    stack_recv,
):
    me_s, me_t = lax.axis_index("sta"), lax.axis_index("tpl")
    dims, steps = sta_offsets(n_sta)
    stations = wave_ref.shape[0]
    n_rows = tpl_ref.shape[0]
    lag_blocks = tpl_ref.shape[2] // BLK
    own_rows = n_rows // n_sta
    seg_blocks = wave_ref.shape[1] // BLK
    wave_blocks = seg_blocks * n_tpl
    time_blocks = wave_blocks - lag_blocks
    out_blocks = time_blocks - 1

    barrier = pltpu.get_barrier_semaphore()
    for step in range(1, n_tpl):
        pl.semaphore_signal(barrier, inc=1, device_id={"tpl": lax.rem(me_t + step, n_tpl)}, device_id_type=MESH)
    for step in steps:
        pl.semaphore_signal(barrier, inc=1, device_id={"sta": peer(me_s, step, dims)}, device_id_type=MESH)

    own_wave = pltpu.make_async_copy(wave_ref, wave_buf.at[me_t], local_sem.at[0])
    own_wave.start()
    tpl_copies = []
    for b in range(lag_blocks):
        tpl_copies.append(
            pltpu.make_async_copy(
                tpl_ref.at[:, :, pl.ds(b * BLK, BLK)], tpl_raw.at[b], local_sem.at[1 + b]
            )
        )
        tpl_copies[-1].start()

    row_view = tpl_raw.reshape(lag_blocks, n_rows * stations, BLK)
    squares = [jnp.zeros((n_rows, BLK), jnp.float32) for _ in range(stations)]
    for b in range(lag_blocks):
        tpl_copies[b].wait()
        rows32[b % 2] = row_view[b].astype(jnp.float32)
        for s in range(stations):
            part = rows32[b % 2, pl.ds(s, n_rows, stride=stations), :]
            squares[s] = squares[s] + part * part
            tpl_split[s, lag_blocks // 2 - 1 - b // 2, :, (b % 2) * BLK : (b % 2 + 1) * BLK] = part.astype(
                jnp.bfloat16
            )

    lane = lax.broadcasted_iota(jnp.int32, (n_rows, BLK), 1)
    weights, gather_at, first_block = [], [], []
    for s in range(stations):
        norm = jnp.sqrt(jnp.sum(squares[s], axis=1, keepdims=True) + EPSILON)
        moved = jnp.transpose(jnp.broadcast_to(mov_ref[s : s + 1, :], (BLK, n_rows)))
        present = jnp.transpose(jnp.broadcast_to(pres_ref[s : s + 1, :].astype(jnp.float32), (BLK, n_rows)))
        weights.append(present / norm)
        position = lane + moved
        gather_at.append(position & (BLK - 1))
        first_block.append(position < BLK)

    pl.semaphore_wait(barrier, n_tpl - 1 + len(steps))
    wave_copies = []
    for step in range(1, n_tpl):
        wave_copies.append(
            pltpu.make_async_remote_copy(
                src_ref=wave_ref,
                dst_ref=wave_buf.at[me_t],
                send_sem=wave_send.at[step - 1],
                recv_sem=wave_recv.at[step - 1],
                device_id={"tpl": lax.rem(me_t + step, n_tpl)},
                device_id_type=MESH,
            )
        )
        wave_copies[-1].start()
    own_wave.wait()
    for copy in wave_copies:
        copy.wait()

    pieces = [
        wave_buf[c // seg_blocks, :, (c % seg_blocks) * BLK : (c % seg_blocks + 1) * BLK] for c in range(wave_blocks)
    ]
    now = jnp.concatenate(pieces, axis=0)
    before = jnp.concatenate([jnp.zeros((stations, BLK), jnp.float32)] + pieces[:-1], axis=0)
    row_lane = lax.broadcasted_iota(jnp.int32, now.shape, 1)
    sums = [now * fir_ref[0, 0], None]
    for i in range(1, fir_ref.shape[1]):
        term = pltpu.roll(jnp.where(row_lane < BLK - i, now, before), i, 1) * fir_ref[0, i]
        sums[i % 2] = term if sums[i % 2] is None else sums[i % 2] + term
    filtered = (sums[0] + sums[1]).astype(jnp.bfloat16).astype(jnp.float32)

    power = filtered * filtered
    after = power
    upto = power
    shift = 1
    while shift < BLK:
        after = after + jnp.where(row_lane < BLK - shift, pltpu.roll(after, BLK - shift, 1), 0.0)
        upto = upto + jnp.where(row_lane >= shift, pltpu.roll(upto, shift, 1), 0.0)
        shift *= 2
    upto = jnp.where(row_lane >= 1, pltpu.roll(upto, 1, 1), 0.0)
    total = jnp.sum(power, axis=1, keepdims=True)
    span = stations * time_blocks
    energy = after[:span] + upto[stations * lag_blocks :]
    for b in range(1, lag_blocks):
        energy = energy + total[stations * b : stations * b + span]
    inverse = 1.0 / jnp.sqrt(energy)

    hankel_at = lax.broadcasted_iota(jnp.int32, (BLK, BLK), 0) + lax.broadcasted_iota(jnp.int32, (BLK, BLK), 1)
    hankel_index = hankel_at & (BLK - 1)
    hankel_first = hankel_at < BLK
    stack = [None] * out_blocks
    for s in range(stations):
        turned = [
            lane_gather(
                jnp.broadcast_to(filtered[stations * c + s : stations * c + s + 1, :], (BLK, BLK)), hankel_index
            )
            for c in range(wave_blocks)
        ]
        blocks = [
            jnp.where(hankel_first, turned[c], turned[c + 1]).astype(jnp.bfloat16) for c in range(wave_blocks - 1)
        ]
        pairs = lag_blocks // 2
        time_pairs = time_blocks // 2
        raw = [None] * time_pairs
        for c in range(pairs + time_pairs - 1):
            tile = jnp.concatenate(
                [
                    jnp.concatenate([blocks[2 * c], blocks[2 * c + 1]], axis=1),
                    jnp.concatenate([blocks[2 * c + 1], blocks[2 * c + 2]], axis=1),
                ],
                axis=0,
            )
            used = [p for p in range(time_pairs) if 0 <= c - p < pairs]
            first = pairs - 1 - (c - used[0])
            rows = tpl_split[s, first : first + len(used)].reshape(len(used) * n_rows, 2 * BLK)
            product = jnp.dot(rows, tile, preferred_element_type=jnp.float32)
            for i, p in enumerate(used):
                part = product[i * n_rows : (i + 1) * n_rows]
                raw[p] = part if raw[p] is None else raw[p] + part
        moved = []
        for b in range(time_blocks):
            scaled = raw[b // 2][:, (b % 2) * BLK : (b % 2 + 1) * BLK] * inverse[stations * b + s : stations * b + s + 1]
            moved.append(lane_gather(scaled, gather_at[s]))
        for b in range(out_blocks):
            term = weights[s] * jnp.where(first_block[s], moved[b], moved[b + 1])
            stack[b] = term if stack[b] is None else stack[b] + term
    send_buf[...] = jnp.concatenate(stack, axis=1).astype(jnp.bfloat16).reshape(send_buf.shape)

    for slot, step in enumerate(steps):
        to = peer(me_s, step, dims)
        pltpu.make_async_remote_copy(
            src_ref=send_buf.at[to],
            dst_ref=recv_buf.at[slot],
            send_sem=stack_send,
            recv_sem=stack_recv,
            device_id={"sta": to},
            device_id_type=MESH,
        ).start()
    own = send_buf[me_s].astype(jnp.float32)
    arrived = recv_buf.at[pl.ds(0, len(steps))]
    pltpu.make_async_copy(arrived, arrived, stack_recv).wait()
    out_ref[0] = own + jnp.sum(arrived[...].astype(jnp.float32), axis=0)
    pltpu.make_async_copy(arrived, arrived, stack_send).wait()


def shards(n_sta, n_tpl, waveform, fir_taps, templates, presence, moveout):
    stations, segment = waveform.shape
    n_rows, _, lags = templates.shape
    own_rows = n_rows // n_sta
    out_len = segment * n_tpl - lags - SHIFT_MOST
    lag_blocks = lags // BLK
    hbm = pl.BlockSpec(memory_space=pl.ANY)
    vmem = pl.BlockSpec(memory_space=pltpu.VMEM)
    return pl.pallas_call(
        functools.partial(kernel, n_sta, n_tpl),
        out_shape=jax.ShapeDtypeStruct((1, own_rows, out_len), jnp.float32),
        in_specs=[hbm, pl.BlockSpec(memory_space=pltpu.SMEM), hbm, vmem, vmem],
        out_specs=vmem,
        scratch_shapes=[
            pltpu.VMEM((n_tpl, stations, segment), jnp.float32),
            pltpu.VMEM((lag_blocks, n_rows, stations, BLK), jnp.bfloat16),
            pltpu.VMEM((2, n_rows * stations, BLK), jnp.float32),
            pltpu.VMEM((stations, lag_blocks // 2, n_rows, 2 * BLK), jnp.bfloat16),
            pltpu.VMEM((n_sta, own_rows, out_len), jnp.bfloat16),
            pltpu.VMEM((n_sta, own_rows, out_len), jnp.bfloat16),
            pltpu.SemaphoreType.DMA((1 + lag_blocks,)),
            pltpu.SemaphoreType.DMA((n_tpl - 1,)),
            pltpu.SemaphoreType.DMA((n_tpl - 1,)),
            pltpu.SemaphoreType.DMA,
            pltpu.SemaphoreType.DMA,
        ],
        compiler_params=pltpu.CompilerParams(collective_id=0, has_side_effects=True),
    )(waveform, fir_taps[None, :], templates, presence.T, moveout.T)


def solution(mesh):
    placed = (P("sta", "tpl"), P(), P("tpl", "sta", None), P("tpl", "sta"), P("tpl", "sta"))
    return jax.shard_map(
        functools.partial(shards, mesh.shape["sta"], mesh.shape["tpl"]),
        mesh=mesh,
        in_specs=placed,
        out_specs=P("tpl", "sta", None),
        check_vma=False,
    )
```

time: 1400 us -> 25.1 us (0.02)
  the two profiles are of different devices: /device:TPU:6 before, /device:TPU:1 now
where the time goes in v1:
time: 25.1 us; the launch traced here: 25 us
  Pallas kernels  23.7 us (94%)
  local copies, waits for them, and re-layouts  1.26 us (5%)
    pallas_call x1, Pallas kernels, shards(): pl.pallas_call(functools.partial(kernel, n_sta, n_tpl), out_shape=jax.Sha...  23.7 us
    unnamed x1, local copies, waits for them, and re-layouts  1.26 us

profile of v1, /device:TPU:1, one launch (start us, length us, event | category | flops | bytes accessed | tf_op | source)
XLA Modules:
  0.0 25.0 jit_solution(17419901279256169122)
XLA Ops:
  0.0 23.7 %shard_map.55 = f32[1,2,384]{2,1,0:T(2,128)} custom-call(f32[2,384]{1,0:T(2,128)} %wave_ref.1, f32[1,64]{1,0:T(1,128)} %bitcast.5, bf16[128,2,1024]{2,1,0:T(2,128)(2,1)} %tpl_ref.1, s32[2,128]{1,0:T(2,128)} %bitcast.3, s32[2,128]{1,0:T(2,128)} %bitcast.4), custom_call_target="tpu_custom_call" | custom-call | tf_op jit(solution)/shard_map/pallas_call | solution.py:225
  23.7 1.3 %copy.7 = f32[1,2,384]{2,1,0:T(2,128)} copy(f32[1,2,384]{2,1,0:T(2,128)} %shard_map.55) | data formatting | bytes 6144

commit v2 on v1

--- a/solution.py
+++ b/solution.py
@@ -17,16 +17,13 @@
     return jnp.take_along_axis(values, index, axis=1, mode="promise_in_bounds")
 
 
-def sta_offsets(n_sta):
-    dims = (2, 8, 4) if n_sta == 64 else (1, n_sta, 1)
-    steps = [
-        (dx, dz, dy) for dx in range(dims[0]) for dz in range(dims[1]) for dy in range(dims[2])
-    ][1:]
-
-    def hops(step):
-        return sum(min(d, n - d) for d, n in zip(step, dims))
-
-    return dims, sorted(steps, key=lambda step: -hops(step))
+def sta_dims(n_sta):
+    return {64: (2, 8, 4), 8: (2, 2, 2), 4: (2, 2, 1)}.get(n_sta, (1, n_sta, 1))
+
+
+def sta_offsets(dims):
+    steps = [(dx, dz, dy) for dx in range(dims[0]) for dz in range(dims[1]) for dy in range(dims[2])][1:]
+    return sorted(steps, key=lambda step: -sum(min(d, n - d) for d, n in zip(step, dims)))
 
 
 def peer(me, step, dims):
@@ -42,10 +39,10 @@
     n_sta,
     n_tpl,
     wave_ref,
-    fir_ref,
+    fir_hbm,
     tpl_ref,
-    pres_ref,
-    mov_ref,
+    pres_hbm,
+    mov_hbm,
     out_ref,
     wave_buf,
     tpl_raw,
@@ -53,14 +50,20 @@
     tpl_split,
     send_buf,
     recv_buf,
+    fir_ref,
+    pres_ref,
+    mov_ref,
     local_sem,
+    small_sem,
+    chain_sem,
     wave_send,
     wave_recv,
     stack_send,
     stack_recv,
 ):
     me_s, me_t = lax.axis_index("sta"), lax.axis_index("tpl")
-    dims, steps = sta_offsets(n_sta)
+    dims = sta_dims(n_sta)
+    steps = sta_offsets(dims)
     stations = wave_ref.shape[0]
     n_rows = tpl_ref.shape[0]
     lag_blocks = tpl_ref.shape[2] // BLK
@@ -70,14 +73,32 @@
     time_blocks = wave_blocks - lag_blocks
     out_blocks = time_blocks - 1
 
+    near_z = [(0, dz, 0) for dz in range(1, dims[1]) if min(dz, dims[1] - dz) <= 2]
+    all_y = [(0, 0, dy) for dy in range(1, dims[2])]
+    all_x = [(dx, 0, 0) for dx in range(1, dims[0])]
+
+    def tell(sem, steps):
+        for step in steps:
+            pl.semaphore_signal(sem, inc=1, device_id={"sta": peer(me_s, step, dims)}, device_id_type=MESH)
+
+    def hear(sem, steps):
+        if steps:
+            pl.semaphore_wait(sem, len(steps))
+
     barrier = pltpu.get_barrier_semaphore()
-    for step in range(1, n_tpl):
+    for step in range(n_tpl - 1, 0, -1):
         pl.semaphore_signal(barrier, inc=1, device_id={"tpl": lax.rem(me_t + step, n_tpl)}, device_id_type=MESH)
-    for step in steps:
-        pl.semaphore_signal(barrier, inc=1, device_id={"sta": peer(me_s, step, dims)}, device_id_type=MESH)
+    tell(barrier, all_x + all_y + near_z)
 
     own_wave = pltpu.make_async_copy(wave_ref, wave_buf.at[me_t], local_sem.at[0])
     own_wave.start()
+    small_copies = [
+        pltpu.make_async_copy(mov_hbm, mov_ref, small_sem.at[0]),
+        pltpu.make_async_copy(pres_hbm, pres_ref, small_sem.at[1]),
+        pltpu.make_async_copy(fir_hbm, fir_ref, small_sem.at[2]),
+    ]
+    for copy in small_copies:
+        copy.start()
     tpl_copies = []
     for b in range(lag_blocks):
         tpl_copies.append(
@@ -86,6 +107,22 @@
             )
         )
         tpl_copies[-1].start()
+
+    pl.semaphore_wait(barrier, n_tpl - 1 + len(all_x + all_y + near_z))
+    wave_copies = []
+    for step in range(1, n_tpl):
+        wave_copies.append(
+            pltpu.make_async_remote_copy(
+                src_ref=wave_ref,
+                dst_ref=wave_buf.at[me_t],
+                send_sem=wave_send.at[step - 1],
+                recv_sem=wave_recv.at[step - 1],
+                device_id={"tpl": lax.rem(me_t + step, n_tpl)},
+                device_id_type=MESH,
+            )
+        )
+        wave_copies[-1].start()
+    tell(chain_sem.at[0], near_z)
 
     row_view = tpl_raw.reshape(lag_blocks, n_rows * stations, BLK)
     squares = [jnp.zeros((n_rows, BLK), jnp.float32) for _ in range(stations)]
@@ -99,6 +136,10 @@
                 jnp.bfloat16
             )
 
+    hear(chain_sem.at[0], near_z)
+    tell(chain_sem.at[1], all_y)
+    for copy in small_copies:
+        copy.wait()
     lane = lax.broadcasted_iota(jnp.int32, (n_rows, BLK), 1)
     weights, gather_at, first_block = [], [], []
     for s in range(stations):
@@ -110,20 +151,6 @@
         gather_at.append(position & (BLK - 1))
         first_block.append(position < BLK)
 
-    pl.semaphore_wait(barrier, n_tpl - 1 + len(steps))
-    wave_copies = []
-    for step in range(1, n_tpl):
-        wave_copies.append(
-            pltpu.make_async_remote_copy(
-                src_ref=wave_ref,
-                dst_ref=wave_buf.at[me_t],
-                send_sem=wave_send.at[step - 1],
-                recv_sem=wave_recv.at[step - 1],
-                device_id={"tpl": lax.rem(me_t + step, n_tpl)},
-                device_id_type=MESH,
-            )
-        )
-        wave_copies[-1].start()
     own_wave.wait()
     for copy in wave_copies:
         copy.wait()
@@ -140,20 +167,24 @@
         sums[i % 2] = term if sums[i % 2] is None else sums[i % 2] + term
     filtered = (sums[0] + sums[1]).astype(jnp.bfloat16).astype(jnp.float32)
 
+    hear(chain_sem.at[1], all_y)
+    tell(chain_sem.at[2], all_x)
+
     power = filtered * filtered
-    after = power
-    upto = power
-    shift = 1
-    while shift < BLK:
-        after = after + jnp.where(row_lane < BLK - shift, pltpu.roll(after, BLK - shift, 1), 0.0)
-        upto = upto + jnp.where(row_lane >= shift, pltpu.roll(upto, shift, 1), 0.0)
-        shift *= 2
-    upto = jnp.where(row_lane >= 1, pltpu.roll(upto, 1, 1), 0.0)
-    total = jnp.sum(power, axis=1, keepdims=True)
+    high = power.astype(jnp.bfloat16)
+    low = (power - high.astype(jnp.float32)).astype(jnp.bfloat16)
+    taken = lax.broadcasted_iota(jnp.int32, (BLK, BLK), 0)
+    at = lax.broadcasted_iota(jnp.int32, (BLK, BLK), 1)
+    rest = jnp.where(taken >= at, 1.0, 0.0)
+    masks = jnp.concatenate([rest, 1.0 - rest, jnp.ones((BLK, BLK), jnp.float32)], axis=1)
+    sums = jnp.dot(
+        jnp.concatenate([high, low], axis=0), masks.astype(jnp.bfloat16), preferred_element_type=jnp.float32
+    )
+    sums = sums[: power.shape[0]] + sums[power.shape[0] :]
     span = stations * time_blocks
-    energy = after[:span] + upto[stations * lag_blocks :]
+    energy = sums[:span, :BLK] + sums[stations * lag_blocks :, BLK : 2 * BLK]
     for b in range(1, lag_blocks):
-        energy = energy + total[stations * b : stations * b + span]
+        energy = energy + sums[stations * b : stations * b + span, 2 * BLK :]
     inverse = 1.0 / jnp.sqrt(energy)
 
     hankel_at = lax.broadcasted_iota(jnp.int32, (BLK, BLK), 0) + lax.broadcasted_iota(jnp.int32, (BLK, BLK), 1)
@@ -197,6 +228,7 @@
             stack[b] = term if stack[b] is None else stack[b] + term
     send_buf[...] = jnp.concatenate(stack, axis=1).astype(jnp.bfloat16).reshape(send_buf.shape)
 
+    hear(chain_sem.at[2], all_x)
     for slot, step in enumerate(steps):
         to = peer(me_s, step, dims)
         pltpu.make_async_remote_copy(
@@ -224,8 +256,8 @@
     vmem = pl.BlockSpec(memory_space=pltpu.VMEM)
     return pl.pallas_call(
         functools.partial(kernel, n_sta, n_tpl),
-        out_shape=jax.ShapeDtypeStruct((1, own_rows, out_len), jnp.float32),
-        in_specs=[hbm, pl.BlockSpec(memory_space=pltpu.SMEM), hbm, vmem, vmem],
+        out_shape=pltpu.VMEM((1, own_rows, out_len), jnp.float32),
+        in_specs=[hbm] * 5,
         out_specs=vmem,
         scratch_shapes=[
             pltpu.VMEM((n_tpl, stations, segment), jnp.float32),
@@ -234,7 +266,12 @@
             pltpu.VMEM((stations, lag_blocks // 2, n_rows, 2 * BLK), jnp.bfloat16),
             pltpu.VMEM((n_sta, own_rows, out_len), jnp.bfloat16),
             pltpu.VMEM((n_sta, own_rows, out_len), jnp.bfloat16),
+            pltpu.SMEM((1, fir_taps.shape[0]), jnp.float32),
+            pltpu.VMEM((stations, n_rows), jnp.int32),
+            pltpu.VMEM((stations, n_rows), jnp.int32),
             pltpu.SemaphoreType.DMA((1 + lag_blocks,)),
+            pltpu.SemaphoreType.DMA((3,)),
+            pltpu.SemaphoreType.REGULAR((3,)),
             pltpu.SemaphoreType.DMA((n_tpl - 1,)),
             pltpu.SemaphoreType.DMA((n_tpl - 1,)),
             pltpu.SemaphoreType.DMA,

time: 25.1 us -> 20.4 us (0.81)
  Pallas kernels: 23.7 us -> 19.7 us
  local copies, waits for them, and re-layouts: 1.26 us -> 0.58 us
    pallas_call x1, Pallas kernels: 23.7 us -> 19.7 us  [shards(): pl.pallas_call(functools.partial(kernel, n_sta, n_tpl), out_shape=pltpu.V...]
    unnamed x1, local copies, waits for them, and re-layouts: 1.26 us -> 0.58 us
where the time goes in v2:
time: 20.4 us; the launch traced here: 20.3 us
  Pallas kernels  19.7 us (97%)
  local copies, waits for them, and re-layouts  0.58 us (3%)
    pallas_call x1, Pallas kernels, shards(): pl.pallas_call(functools.partial(kernel, n_sta, n_tpl), out_shape=pltpu.V...  19.7 us
    unnamed x1, local copies, waits for them, and re-layouts  0.58 us

profile of v2, /device:TPU:1, one launch (start us, length us, event | category | flops | bytes accessed | tf_op | source)
XLA Modules:
  0.0 20.3 jit_solution(6126258740450738104)
XLA Ops:
  0.0 19.7 %shard_map.55 = f32[1,2,384]{2,1,0:T(2,128)S(1)} custom-call(f32[2,384]{1,0:T(2,128)} %wave_ref.1, f32[1,64]{1,0:T(1,128)} %bitcast.5, bf16[128,2,1024]{2,1,0:T(2,128)(2,1)} %tpl_ref.1, s32[2,128]{1,0:T(2,128)} %bitcast.3, s32[2,128]{1,0:T(2,128)} %bitcast.4), custom_call_target="tpu_custom_call" | custom-call | tf_op jit(solution)/shard_map/pallas_call | solution.py:257
  19.7 0.6 %copy.7 = f32[1,2,384]{2,1,0:T(2,128)} copy(f32[1,2,384]{2,1,0:T(2,128)S(1)} %shard_map.55) | data formatting | bytes 6144

commit v3 on v2

--- a/solution.py
+++ b/solution.py
@@ -73,22 +73,27 @@
     time_blocks = wave_blocks - lag_blocks
     out_blocks = time_blocks - 1
 
-    near_z = [(0, dz, 0) for dz in range(1, dims[1]) if min(dz, dims[1] - dz) <= 2]
-    all_y = [(0, 0, dy) for dy in range(1, dims[2])]
-    all_x = [(dx, 0, 0) for dx in range(1, dims[0])]
+    def ring(axis, distance):
+        hops = {distance % dims[axis], -distance % dims[axis]} - {0}
+        return [tuple(hop if i == axis else 0 for i in range(3)) for hop in sorted(hops)]
+
+    near = ring(0, 1) + ring(2, 1) + ring(1, 1)
+    chain = [ring(1, 1), ring(1, 2), ring(2, 1), ring(2, 1), ring(0, 1)]
 
     def tell(sem, steps):
         for step in steps:
             pl.semaphore_signal(sem, inc=1, device_id={"sta": peer(me_s, step, dims)}, device_id_type=MESH)
 
-    def hear(sem, steps):
-        if steps:
-            pl.semaphore_wait(sem, len(steps))
+    def hear(stage):
+        if chain[stage]:
+            pl.semaphore_wait(chain_sem.at[stage], len(chain[stage]))
+        if stage + 1 < len(chain):
+            tell(chain_sem.at[stage + 1], chain[stage + 1])
 
     barrier = pltpu.get_barrier_semaphore()
     for step in range(n_tpl - 1, 0, -1):
         pl.semaphore_signal(barrier, inc=1, device_id={"tpl": lax.rem(me_t + step, n_tpl)}, device_id_type=MESH)
-    tell(barrier, all_x + all_y + near_z)
+    tell(barrier, near)
 
     own_wave = pltpu.make_async_copy(wave_ref, wave_buf.at[me_t], local_sem.at[0])
     own_wave.start()
@@ -108,12 +113,13 @@
         )
         tpl_copies[-1].start()
 
-    pl.semaphore_wait(barrier, n_tpl - 1 + len(all_x + all_y + near_z))
+    pl.semaphore_wait(barrier, n_tpl - 1 + len(near))
+    own_wave.wait()
     wave_copies = []
     for step in range(1, n_tpl):
         wave_copies.append(
             pltpu.make_async_remote_copy(
-                src_ref=wave_ref,
+                src_ref=wave_buf.at[me_t],
                 dst_ref=wave_buf.at[me_t],
                 send_sem=wave_send.at[step - 1],
                 recv_sem=wave_recv.at[step - 1],
@@ -122,11 +128,13 @@
             )
         )
         wave_copies[-1].start()
-    tell(chain_sem.at[0], near_z)
+    tell(chain_sem.at[0], chain[0])
 
     row_view = tpl_raw.reshape(lag_blocks, n_rows * stations, BLK)
     squares = [jnp.zeros((n_rows, BLK), jnp.float32) for _ in range(stations)]
     for b in range(lag_blocks):
+        if b == lag_blocks // 2:
+            hear(0)
         tpl_copies[b].wait()
         rows32[b % 2] = row_view[b].astype(jnp.float32)
         for s in range(stations):
@@ -136,8 +144,6 @@
                 jnp.bfloat16
             )
 
-    hear(chain_sem.at[0], near_z)
-    tell(chain_sem.at[1], all_y)
     for copy in small_copies:
         copy.wait()
     lane = lax.broadcasted_iota(jnp.int32, (n_rows, BLK), 1)
@@ -151,7 +157,7 @@
         gather_at.append(position & (BLK - 1))
         first_block.append(position < BLK)
 
-    own_wave.wait()
+    hear(1)
     for copy in wave_copies:
         copy.wait()
 
@@ -166,9 +172,6 @@
         term = pltpu.roll(jnp.where(row_lane < BLK - i, now, before), i, 1) * fir_ref[0, i]
         sums[i % 2] = term if sums[i % 2] is None else sums[i % 2] + term
     filtered = (sums[0] + sums[1]).astype(jnp.bfloat16).astype(jnp.float32)
-
-    hear(chain_sem.at[1], all_y)
-    tell(chain_sem.at[2], all_x)
 
     power = filtered * filtered
     high = power.astype(jnp.bfloat16)
@@ -187,19 +190,33 @@
         energy = energy + sums[stations * b : stations * b + span, 2 * BLK :]
     inverse = 1.0 / jnp.sqrt(energy)
 
-    hankel_at = lax.broadcasted_iota(jnp.int32, (BLK, BLK), 0) + lax.broadcasted_iota(jnp.int32, (BLK, BLK), 1)
+    tall = 16
+    hankel_at = lax.broadcasted_iota(jnp.int32, (tall, BLK), 0) + lax.broadcasted_iota(jnp.int32, (tall, BLK), 1)
     hankel_index = hankel_at & (BLK - 1)
     hankel_first = hankel_at < BLK
+    tall_lane = lax.broadcasted_iota(jnp.int32, (tall, BLK), 1)
     stack = [None] * out_blocks
     for s in range(stations):
         turned = [
             lane_gather(
-                jnp.broadcast_to(filtered[stations * c + s : stations * c + s + 1, :], (BLK, BLK)), hankel_index
-            )
+                jnp.broadcast_to(filtered[stations * c + s : stations * c + s + 1, :], (tall, BLK)), hankel_index
+            )
+            for c in range(wave_blocks)
+        ]
+        heads = [
+            jnp.where(hankel_first, turned[c], turned[min(c + 1, wave_blocks - 1)]).astype(jnp.bfloat16)
             for c in range(wave_blocks)
         ]
         blocks = [
-            jnp.where(hankel_first, turned[c], turned[c + 1]).astype(jnp.bfloat16) for c in range(wave_blocks - 1)
+            jnp.concatenate(
+                [heads[c]]
+                + [
+                    pltpu.roll(jnp.where(tall_lane < q, heads[c + 1], heads[c]), BLK - q, 1)
+                    for q in range(tall, BLK, tall)
+                ],
+                axis=0,
+            )
+            for c in range(wave_blocks - 1)
         ]
         pairs = lag_blocks // 2
         time_pairs = time_blocks // 2
@@ -219,6 +236,7 @@
             for i, p in enumerate(used):
                 part = product[i * n_rows : (i + 1) * n_rows]
                 raw[p] = part if raw[p] is None else raw[p] + part
+        hear(2 + s) if stations == 2 else None
         moved = []
         for b in range(time_blocks):
             scaled = raw[b // 2][:, (b % 2) * BLK : (b % 2 + 1) * BLK] * inverse[stations * b + s : stations * b + s + 1]
@@ -228,7 +246,7 @@
             stack[b] = term if stack[b] is None else stack[b] + term
     send_buf[...] = jnp.concatenate(stack, axis=1).astype(jnp.bfloat16).reshape(send_buf.shape)
 
-    hear(chain_sem.at[2], all_x)
+    hear(4)
     for slot, step in enumerate(steps):
         to = peer(me_s, step, dims)
         pltpu.make_async_remote_copy(
@@ -271,7 +289,7 @@
             pltpu.VMEM((stations, n_rows), jnp.int32),
             pltpu.SemaphoreType.DMA((1 + lag_blocks,)),
             pltpu.SemaphoreType.DMA((3,)),
-            pltpu.SemaphoreType.REGULAR((3,)),
+            pltpu.SemaphoreType.REGULAR((5,)),
             pltpu.SemaphoreType.DMA((n_tpl - 1,)),
             pltpu.SemaphoreType.DMA((n_tpl - 1,)),
             pltpu.SemaphoreType.DMA,

time: 20.4 us -> 22.7 us (1.11); the launches traced: 20.3 us -> 22.3 us
  Pallas kernels: 19.7 us -> 21.7 us
    pallas_call x1, Pallas kernels: 19.7 us -> 21.7 us  [shards(): pl.pallas_call(functools.partial(kernel, n_sta, n_tpl), out_shape=pltpu.V...]
where the time goes in v3:
time: 22.7 us; the launch traced here: 22.3 us
  Pallas kernels  21.7 us (96%)
  local copies, waits for them, and re-layouts  0.58 us (3%)
    pallas_call x1, Pallas kernels, shards(): pl.pallas_call(functools.partial(kernel, n_sta, n_tpl), out_shape=pltpu.V...  21.7 us
    unnamed x1, local copies, waits for them, and re-layouts  0.58 us

profile of v3, /device:TPU:1, one launch (start us, length us, event | category | flops | bytes accessed | tf_op | source)
XLA Modules:
  0.0 22.3 jit_solution(4442118995369754439)
XLA Ops:
  0.0 21.7 %shard_map.55 = f32[1,2,384]{2,1,0:T(2,128)S(1)} custom-call(f32[2,384]{1,0:T(2,128)} %wave_ref.1, f32[1,64]{1,0:T(1,128)} %bitcast.5, bf16[128,2,1024]{2,1,0:T(2,128)(2,1)} %tpl_ref.1, s32[2,128]{1,0:T(2,128)} %bitcast.3, s32[2,128]{1,0:T(2,128)} %bitcast.4), custom_call_target="tpu_custom_call" | custom-call | tf_op jit(solution)/shard_map/pallas_call | solution.py:275
  21.8 0.6 %copy.7 = f32[1,2,384]{2,1,0:T(2,128)} copy(f32[1,2,384]{2,1,0:T(2,128)S(1)} %shard_map.55) | data formatting | bytes 6144

commit v4 on v3

--- a/solution.py
+++ b/solution.py
@@ -23,7 +23,8 @@
 
 def sta_offsets(dims):
     steps = [(dx, dz, dy) for dx in range(dims[0]) for dz in range(dims[1]) for dy in range(dims[2])][1:]
-    return sorted(steps, key=lambda step: -sum(min(d, n - d) for d, n in zip(step, dims)))
+    far = {step: sum(min(d, n - d) for d, n in zip(step, dims)) for step in steps}
+    return {step: far[step] for step in sorted(steps, key=lambda step: -far[step])}
 
 
 def peer(me, step, dims):
@@ -73,12 +74,11 @@
     time_blocks = wave_blocks - lag_blocks
     out_blocks = time_blocks - 1
 
-    def ring(axis, distance):
-        hops = {distance % dims[axis], -distance % dims[axis]} - {0}
-        return [tuple(hop if i == axis else 0 for i in range(3)) for hop in sorted(hops)]
-
-    near = ring(0, 1) + ring(2, 1) + ring(1, 1)
-    chain = [ring(1, 1), ring(1, 2), ring(2, 1), ring(2, 1), ring(0, 1)]
+    def ring(distance):
+        return [step for step, hops in steps.items() if hops == distance]
+
+    near = ring(1)
+    chain = [ring(1), ring(2), ring(3)]
 
     def tell(sem, steps):
         for step in steps:
@@ -133,8 +133,6 @@
     row_view = tpl_raw.reshape(lag_blocks, n_rows * stations, BLK)
     squares = [jnp.zeros((n_rows, BLK), jnp.float32) for _ in range(stations)]
     for b in range(lag_blocks):
-        if b == lag_blocks // 2:
-            hear(0)
         tpl_copies[b].wait()
         rows32[b % 2] = row_view[b].astype(jnp.float32)
         for s in range(stations):
@@ -144,6 +142,7 @@
                 jnp.bfloat16
             )
 
+    hear(0)
     for copy in small_copies:
         copy.wait()
     lane = lax.broadcasted_iota(jnp.int32, (n_rows, BLK), 1)
@@ -236,7 +235,6 @@
             for i, p in enumerate(used):
                 part = product[i * n_rows : (i + 1) * n_rows]
                 raw[p] = part if raw[p] is None else raw[p] + part
-        hear(2 + s) if stations == 2 else None
         moved = []
         for b in range(time_blocks):
             scaled = raw[b // 2][:, (b % 2) * BLK : (b % 2 + 1) * BLK] * inverse[stations * b + s : stations * b + s + 1]
@@ -246,7 +244,7 @@
             stack[b] = term if stack[b] is None else stack[b] + term
     send_buf[...] = jnp.concatenate(stack, axis=1).astype(jnp.bfloat16).reshape(send_buf.shape)
 
-    hear(4)
+    hear(2)
     for slot, step in enumerate(steps):
         to = peer(me_s, step, dims)
         pltpu.make_async_remote_copy(
@@ -289,7 +287,7 @@
             pltpu.VMEM((stations, n_rows), jnp.int32),
             pltpu.SemaphoreType.DMA((1 + lag_blocks,)),
             pltpu.SemaphoreType.DMA((3,)),
-            pltpu.SemaphoreType.REGULAR((5,)),
+            pltpu.SemaphoreType.REGULAR((3,)),
             pltpu.SemaphoreType.DMA((n_tpl - 1,)),
             pltpu.SemaphoreType.DMA((n_tpl - 1,)),
             pltpu.SemaphoreType.DMA,

time: 22.7 us -> 22.3 us (0.982); the launches traced: 22.3 us -> 22.2 us
  no operation moved by 1% of the time
where the time goes in v4:
time: 22.3 us; the launch traced here: 22.2 us
  Pallas kernels  21.7 us (97%)
  local copies, waits for them, and re-layouts  0.58 us (3%)
    pallas_call x1, Pallas kernels, shards(): pl.pallas_call(functools.partial(kernel, n_sta, n_tpl), out_shape=pltpu.V...  21.7 us
    unnamed x1, local copies, waits for them, and re-layouts  0.58 us

profile of v4, /device:TPU:1, one launch (start us, length us, event | category | flops | bytes accessed | tf_op | source)
XLA Modules:
  0.0 22.2 jit_solution(10829062747959357793)
XLA Ops:
  0.0 21.7 %shard_map.55 = f32[1,2,384]{2,1,0:T(2,128)S(1)} custom-call(f32[2,384]{1,0:T(2,128)} %wave_ref.1, f32[1,64]{1,0:T(1,128)} %bitcast.5, bf16[128,2,1024]{2,1,0:T(2,128)(2,1)} %tpl_ref.1, s32[2,128]{1,0:T(2,128)} %bitcast.3, s32[2,128]{1,0:T(2,128)} %bitcast.4), custom_call_target="tpu_custom_call" | custom-call | tf_op jit(solution)/shard_map/pallas_call | solution.py:273
  21.7 0.6 %copy.7 = f32[1,2,384]{2,1,0:T(2,128)} copy(f32[1,2,384]{2,1,0:T(2,128)S(1)} %shard_map.55) | data formatting | bytes 6144

commit v5 on v4

--- a/solution.py
+++ b/solution.py
@@ -21,19 +21,16 @@
     return {64: (2, 8, 4), 8: (2, 2, 2), 4: (2, 2, 1)}.get(n_sta, (1, n_sta, 1))
 
 
-def sta_offsets(dims):
-    steps = [(dx, dz, dy) for dx in range(dims[0]) for dz in range(dims[1]) for dy in range(dims[2])][1:]
-    far = {step: sum(min(d, n - d) for d, n in zip(step, dims)) for step in steps}
-    return {step: far[step] for step in sorted(steps, key=lambda step: -far[step])}
-
-
-def peer(me, step, dims):
+def places(me, dims):
     x, rest = me // (dims[1] * dims[2]), me % (dims[1] * dims[2])
     z, y = rest // dims[2], rest % dims[2]
-    x = (x + step[0]) % dims[0]
-    z = (z + step[1]) % dims[1]
-    y = (y + step[2]) % dims[2]
-    return (x * dims[1] + z) * dims[2] + y
+    xs = [((x + d) % dims[0]) * (dims[1] * dims[2]) for d in range(dims[0])]
+    ys = [(y + d) % dims[2] for d in range(dims[2])]
+    return z, lambda dx, dy, at: xs[dx] + ys[dy] + at * dims[2]
+
+
+def nearest(z, planes, n):
+    return min(planes, key=lambda p: min((z - p) % n, (p - z) % n))
 
 
 def kernel(
@@ -64,7 +61,12 @@
 ):
     me_s, me_t = lax.axis_index("sta"), lax.axis_index("tpl")
     dims = sta_dims(n_sta)
-    steps = sta_offsets(dims)
+    me_z, place = places(me_s, dims)
+    early = list(range(max(1, dims[1] // 4)))
+    late = list(range(len(early), dims[1]))
+    plane = [(dx, dy) for dx in range(dims[0]) for dy in range(dims[2])]
+    plane.sort(key=lambda step: -sum(min(d, n - d) for d, n in zip(step, (dims[0], dims[2]))))
+    is_early = me_z < len(early)
     stations = wave_ref.shape[0]
     n_rows = tpl_ref.shape[0]
     lag_blocks = tpl_ref.shape[2] // BLK
@@ -74,26 +76,25 @@
     time_blocks = wave_blocks - lag_blocks
     out_blocks = time_blocks - 1
 
-    def ring(distance):
-        return [step for step, hops in steps.items() if hops == distance]
-
-    near = ring(1)
-    chain = [ring(1), ring(2), ring(3)]
-
-    def tell(sem, steps):
-        for step in steps:
-            pl.semaphore_signal(sem, inc=1, device_id={"sta": peer(me_s, step, dims)}, device_id_type=MESH)
-
-    def hear(stage):
-        if chain[stage]:
-            pl.semaphore_wait(chain_sem.at[stage], len(chain[stage]))
-        if stage + 1 < len(chain):
-            tell(chain_sem.at[stage + 1], chain[stage + 1])
+    def each(planes, do):
+        for step in plane:
+            for at in planes:
+                to = place(*step, at)
+                if step == (0, 0):
+                    pl.when(me_z != at)(functools.partial(do, to))
+                else:
+                    do(to)
+
+    def tell(sem, to):
+        pl.semaphore_signal(sem, inc=1, device_id={"sta": to}, device_id_type=MESH)
 
     barrier = pltpu.get_barrier_semaphore()
     for step in range(n_tpl - 1, 0, -1):
         pl.semaphore_signal(barrier, inc=1, device_id={"tpl": lax.rem(me_t + step, n_tpl)}, device_id_type=MESH)
-    tell(barrier, near)
+
+    @pl.when(is_early)
+    def _():
+        each(late + early, functools.partial(tell, barrier))
 
     own_wave = pltpu.make_async_copy(wave_ref, wave_buf.at[me_t], local_sem.at[0])
     own_wave.start()
@@ -113,7 +114,8 @@
         )
         tpl_copies[-1].start()
 
-    pl.semaphore_wait(barrier, n_tpl - 1 + len(near))
+    n_early = len(plane) * len(early)
+    pl.semaphore_wait(barrier, n_tpl - 1 + n_early - is_early.astype(jnp.int32))
     own_wave.wait()
     wave_copies = []
     for step in range(1, n_tpl):
@@ -128,7 +130,10 @@
             )
         )
         wave_copies[-1].start()
-    tell(chain_sem.at[0], chain[0])
+    @pl.when(jnp.logical_not(is_early))
+    def _():
+        each(early, functools.partial(tell, chain_sem.at[0]))
+
 
     row_view = tpl_raw.reshape(lag_blocks, n_rows * stations, BLK)
     squares = [jnp.zeros((n_rows, BLK), jnp.float32) for _ in range(stations)]
@@ -142,7 +147,6 @@
                 jnp.bfloat16
             )
 
-    hear(0)
     for copy in small_copies:
         copy.wait()
     lane = lax.broadcasted_iota(jnp.int32, (n_rows, BLK), 1)
@@ -156,9 +160,8 @@
         gather_at.append(position & (BLK - 1))
         first_block.append(position < BLK)
 
-    hear(1)
     for copy in wave_copies:
-        copy.wait()
+        copy.wait_recv()
 
     pieces = [
         wave_buf[c // seg_blocks, :, (c % seg_blocks) * BLK : (c % seg_blocks + 1) * BLK] for c in range(wave_blocks)
@@ -244,21 +247,37 @@
             stack[b] = term if stack[b] is None else stack[b] + term
     send_buf[...] = jnp.concatenate(stack, axis=1).astype(jnp.bfloat16).reshape(send_buf.shape)
 
-    hear(2)
-    for slot, step in enumerate(steps):
-        to = peer(me_s, step, dims)
+    def send(to):
         pltpu.make_async_remote_copy(
             src_ref=send_buf.at[to],
-            dst_ref=recv_buf.at[slot],
+            dst_ref=recv_buf.at[me_s],
             send_sem=stack_send,
             recv_sem=stack_recv,
             device_id={"sta": to},
             device_id_type=MESH,
         ).start()
-    own = send_buf[me_s].astype(jnp.float32)
-    arrived = recv_buf.at[pl.ds(0, len(steps))]
+
+    each(early, send)
+    recv_buf[me_s] = send_buf[me_s]
+
+    @pl.when(is_early)
+    def _():
+        pl.semaphore_wait(chain_sem.at[0], len(plane) * len(late))
+        for at in late:
+            @pl.when(me_z == nearest(at, early, dims[1]))
+            def _():
+                tell(chain_sem.at[1], place(0, 0, at))
+
+    @pl.when(jnp.logical_not(is_early))
+    def _():
+        pl.semaphore_wait(chain_sem.at[1], 1)
+
+    each(late, send)
+    arrived = recv_buf.at[pl.ds(0, n_sta - 1)]
     pltpu.make_async_copy(arrived, arrived, stack_recv).wait()
-    out_ref[0] = own + jnp.sum(arrived[...].astype(jnp.float32), axis=0)
+    out_ref[0] = jnp.sum(recv_buf[...].astype(jnp.float32), axis=0)
+    for copy in wave_copies:
+        copy.wait_send()
     pltpu.make_async_copy(arrived, arrived, stack_send).wait()
 
 
@@ -287,7 +306,7 @@
             pltpu.VMEM((stations, n_rows), jnp.int32),
             pltpu.SemaphoreType.DMA((1 + lag_blocks,)),
             pltpu.SemaphoreType.DMA((3,)),
-            pltpu.SemaphoreType.REGULAR((3,)),
+            pltpu.SemaphoreType.REGULAR((2,)),
             pltpu.SemaphoreType.DMA((n_tpl - 1,)),
             pltpu.SemaphoreType.DMA((n_tpl - 1,)),
             pltpu.SemaphoreType.DMA,

time: 22.3 us -> 20.3 us (0.910)
  Pallas kernels: 21.7 us -> 19.4 us
    pallas_call x1, Pallas kernels: 21.7 us -> 19.4 us  [shards(): pl.pallas_call(functools.partial(kernel, n_sta, n_tpl), out_shape=pltpu.V...]
where the time goes in v5:
time: 20.3 us; the launch traced here: 20 us
  Pallas kernels  19.4 us (96%)
  local copies, waits for them, and re-layouts  0.58 us (3%)
    pallas_call x1, Pallas kernels, shards(): pl.pallas_call(functools.partial(kernel, n_sta, n_tpl), out_shape=pltpu.V...  19.4 us
    unnamed x1, local copies, waits for them, and re-layouts  0.58 us

profile of v5, /device:TPU:1, one launch (start us, length us, event | category | flops | bytes accessed | tf_op | source)
XLA Modules:
  0.0 20.0 jit_solution(3517379976135416386)
XLA Ops:
  0.0 19.4 %shard_map.55 = f32[1,2,384]{2,1,0:T(2,128)S(1)} custom-call(f32[2,384]{1,0:T(2,128)} %wave_ref.1, f32[1,64]{1,0:T(1,128)} %bitcast.5, bf16[128,2,1024]{2,1,0:T(2,128)(2,1)} %tpl_ref.1, s32[2,128]{1,0:T(2,128)} %bitcast.3, s32[2,128]{1,0:T(2,128)} %bitcast.4), custom_call_target="tpu_custom_call" | custom-call | tf_op jit(solution)/shard_map/pallas_call | solution.py:292
  19.5 0.6 %copy.7 = f32[1,2,384]{2,1,0:T(2,128)} copy(f32[1,2,384]{2,1,0:T(2,128)S(1)} %shard_map.55) | data formatting | bytes 6144
